TPU v7x, 32 devices: a whole 2x2x4 slice. The times are simulated.
32 devices in a mesh: tm: 2 (over core), loan: 8 (over z, y), cov: 2 (over x).
Axes of the slice: x: 2, y: 2, z: 4, core: 2. Of those that a mesh axis runs over, the one named last changes fastest.
Arguments:
- covars: float32 [65536, 1024], P(('tm', 'loan'), 'cov'), may hold values from -6 to 6
- events: int32 [65536], P(('tm', 'loan')), may hold values 0 or 1
- group: int32 [65536], P(('tm', 'loan')), may hold values from 0 to 511, as said below
- counts: int32 [16], P(('tm', 'loan')), may hold values from 1024 to 4096
- beta: float32 [1024], P('cov'), may hold values from -0.1875 to 0.1875
- vecs: float32 [2, 1024], P(None, 'cov'), may hold values from -12 to 12
Outputs:
- hessvec: float32 [2, 1024], P(None, 'cov')
Inputs may be any that keep to these rules, and one draw needn't show every extreme that they name: `group`: block b holds tie groups of time shard b // (16 // (512 // 256)) only: from 256 times the shard's index to 256 more minus one; the first 256 rows of every block hold each of these groups once.
All inputs are finite; a program needn't handle non-finite values. No bound on the sum of `events` on one device may be relied on, other than what follows from the above.
Results may differ from a plain program's by a relative error of at most 0.00028.
Values sent between devices are 32-bit elements; how exact they have to be, the bound alone decides.
No kernel may reach another device: no remote copies, remote signals or barrier semaphores. Data moves between devices by JAX's collectives and lax.ppermute only.
A program may use at most 64 MiB of HBM per device.

v0:
```python
import jax
import jax.numpy as jnp
from jax import lax
from jax.sharding import PartitionSpec as P

G_SH = 256
exact_mode = lax.Precision.HIGHEST


def carried_in(value, axis, join, neutral, backward):
    count, mine = (lax.axis_size(axis), lax.axis_index(axis))
    pieces = lax.all_gather(value, axis)
    if backward:
        pieces = pieces[::-1]
        mine = count - 1 - mine
    running = jnp.full_like(value, 0) + jnp.asarray(neutral, value.dtype)

    def hop(position, running):
        longer = join(running, pieces[position])
        return jnp.where(position < mine, longer, running)

    return lax.fori_loop(0, count - 1, hop, running)


def add_trees(earlier, later):
    return jax.tree.map(jnp.add, earlier, later)


def sweep(trips, block, update, initial):

    def advance(trip_index, carry):
        return update(trip_index * block, carry)

    return lax.fori_loop(0, trips, advance, initial)


def per_device(covars, events, group, counts, beta, vecs):
    row_total, col_width = covars.shape
    block = min(512, row_total)
    shard = lax.axis_index("tm")
    records_all = row_total * lax.axis_size("tm") * lax.axis_size("loan")
    row_count = counts[0]
    trips = row_total // block
    coeffs = jnp.concatenate([beta[None, :], vecs], axis=0)

    def predict(start, partial_value):
        piece = lax.dynamic_slice_in_dim(covars, start, block, 0)
        values = lax.dot_general(coeffs, piece, (((1,), (1,)), ((), ())), precision=exact_mode)
        return lax.dynamic_update_slice_in_dim(partial_value, values, start, 1)

    partial_value = sweep(trips, block, predict, jnp.zeros((3, row_total), jnp.float32))
    linear = lax.psum(partial_value, "cov")
    valid = (jnp.arange(row_total, dtype=jnp.int32) < row_count).astype(jnp.float32)
    weight = valid * jnp.exp(linear[0])
    projected = linear[1:3]
    died = valid * events.astype(jnp.float32)
    per_record = jnp.concatenate(
        [weight[None, :], weight[None, :] * projected, died[None, :]], axis=0
    )
    local_group = group - shard * G_SH
    group_iota = jnp.arange(G_SH, dtype=jnp.int32)
    upper_ones = (group_iota[:, None] >= group_iota[None, :]).astype(jnp.float32)

    def indicator(start):
        labels = lax.dynamic_slice_in_dim(local_group, start, block, 0)
        return (labels[:, None] == group_iota[None, :]).astype(jnp.float32)

    def tally(start, stats_acc):
        member = indicator(start)
        values = lax.dynamic_slice_in_dim(per_record, start, block, 1)
        return stats_acc + jnp.dot(values, member, precision=exact_mode)

    stats_local = sweep(trips, block, tally, jnp.zeros((4, G_SH), jnp.float32))
    totals = lax.psum(stats_local, "loan")
    sums = totals[:3]
    died_grp = totals[3]
    tail = carried_in(jnp.sum(sums, axis=1), "tm", add_trees, jnp.zeros((3,), jnp.float32), True)
    risk = jnp.dot(sums, upper_ones, precision=exact_mode) + tail[:, None]
    ratios = jnp.concatenate(
        [
            (died_grp / risk[0])[None, :],
            died_grp[None, :] * risk[1:3] / (risk[0] * risk[0])[None, :],
        ],
        axis=0,
    )
    head = carried_in(jnp.sum(ratios, axis=1), "tm", add_trees, jnp.zeros((3,), jnp.float32), False)
    cumulative = jnp.dot(ratios, upper_ones.T, precision=exact_mode) + head[:, None]

    def assemble(start, product_acc):
        member = indicator(start)
        looked = lax.dot_general(cumulative, member, (((1,), (1,)), ((), ())), precision=exact_mode)
        weight_part = lax.dynamic_slice_in_dim(weight, start, block, 0)
        proj_part = lax.dynamic_slice_in_dim(projected, start, block, 1)
        resid = weight_part[None, :] * (proj_part * looked[0][None, :] - looked[1:3])
        piece = lax.dynamic_slice_in_dim(covars, start, block, 0)
        return product_acc + jnp.dot(resid, piece, precision=exact_mode)

    parts = sweep(trips, block, assemble, jnp.zeros((2, col_width), jnp.float32))
    product = lax.psum(parts, ("tm", "loan"))
    return product / records_all


def solution(mesh):
    return jax.shard_map(
        per_device,
        mesh=mesh,
        in_specs=(
            P(("tm", "loan"), "cov"),
            P(("tm", "loan")),
            P(("tm", "loan")),
            P(("tm", "loan")),
            P("cov"),
            P(None, "cov"),
        ),
        out_specs=P(None, "cov"),
        check_vma=False,
    )
```

profile of v0, /device:TPU:0, one launch (start us, length us, event | category | flops | bytes accessed | tf_op | source)
XLA Modules:
  0.0 113.7 jit_solution(10290802062483819432)
XLA Ops:
  1.4 17.8 %while.51 = (s32[]{:T(128)}, f32[3,4096]{1,0:T(4,128)S(1)}, f32[4096,512]{1,0:T(8,128)}, f32[3,512]{1,0:T(4,128)S(1)}, s32[]{:T(128)}, /*index=5*/s32[]{:T(128)}, s32[]{:T(128)}, s32[]{:T(128)}) while((s32[]{:T(128)}, f32[3,4096]{1,0:T(4,128)S(1)}, f32[4096,512]{1,0:T(8,128)}, f32[3,512]{1,0:T(4,128)S(1)}, s32[]{:T(128)}, ...), condition=%wide.region_1.0_spmd, body=%wide.region_0.0_spmd.sunk | while | flops 9437190 | bytes 1066115 | solution.py:34
  1.4 2.2 %fusion.35 = f32[3,4096]{1,0:T(4,128)S(1)} fusion(f32[3,4096]{1,0:T(4,128)S(1)} %get-tuple-element.532, s32[]{:T(128)S(6)} %select_n.77, f32[3,512]{1,0:T(4,128)S(1)} %get-tuple-element.542, f32[4096,512]{1,0:T(8,128)} %get-tuple-element.541), kind=kOutput, calls=%fused_computation.3.clone.1 | convolution fusion | flops 9437184 | bytes 1065984 | tf_op jit(solution)/shard_map/while/body/eval_jaxpr/dot_general | solution.py:48
  3.6 2.2 %fusion.35 = f32[3,4096]{1,0:T(4,128)S(1)} fusion(f32[3,4096]{1,0:T(4,128)S(1)} %get-tuple-element.532, s32[]{:T(128)S(6)} %select_n.77, f32[3,512]{1,0:T(4,128)S(1)} %get-tuple-element.542, f32[4096,512]{1,0:T(8,128)} %get-tuple-element.541), kind=kOutput, calls=%fused_computation.3.clone.1 | convolution fusion | flops 9437184 | bytes 1065984 | tf_op jit(solution)/shard_map/while/body/eval_jaxpr/dot_general | solution.py:48
  5.8 2.2 %fusion.35 = f32[3,4096]{1,0:T(4,128)S(1)} fusion(f32[3,4096]{1,0:T(4,128)S(1)} %get-tuple-element.532, s32[]{:T(128)S(6)} %select_n.77, f32[3,512]{1,0:T(4,128)S(1)} %get-tuple-element.542, f32[4096,512]{1,0:T(8,128)} %get-tuple-element.541), kind=kOutput, calls=%fused_computation.3.clone.1 | convolution fusion | flops 9437184 | bytes 1065984 | tf_op jit(solution)/shard_map/while/body/eval_jaxpr/dot_general | solution.py:48
  8.0 2.2 %fusion.35 = f32[3,4096]{1,0:T(4,128)S(1)} fusion(f32[3,4096]{1,0:T(4,128)S(1)} %get-tuple-element.532, s32[]{:T(128)S(6)} %select_n.77, f32[3,512]{1,0:T(4,128)S(1)} %get-tuple-element.542, f32[4096,512]{1,0:T(8,128)} %get-tuple-element.541), kind=kOutput, calls=%fused_computation.3.clone.1 | convolution fusion | flops 9437184 | bytes 1065984 | tf_op jit(solution)/shard_map/while/body/eval_jaxpr/dot_general | solution.py:48
  10.3 2.2 %fusion.35 = f32[3,4096]{1,0:T(4,128)S(1)} fusion(f32[3,4096]{1,0:T(4,128)S(1)} %get-tuple-element.532, s32[]{:T(128)S(6)} %select_n.77, f32[3,512]{1,0:T(4,128)S(1)} %get-tuple-element.542, f32[4096,512]{1,0:T(8,128)} %get-tuple-element.541), kind=kOutput, calls=%fused_computation.3.clone.1 | convolution fusion | flops 9437184 | bytes 1065984 | tf_op jit(solution)/shard_map/while/body/eval_jaxpr/dot_general | solution.py:48
  12.5 2.2 %fusion.35 = f32[3,4096]{1,0:T(4,128)S(1)} fusion(f32[3,4096]{1,0:T(4,128)S(1)} %get-tuple-element.532, s32[]{:T(128)S(6)} %select_n.77, f32[3,512]{1,0:T(4,128)S(1)} %get-tuple-element.542, f32[4096,512]{1,0:T(8,128)} %get-tuple-element.541), kind=kOutput, calls=%fused_computation.3.clone.1 | convolution fusion | flops 9437184 | bytes 1065984 | tf_op jit(solution)/shard_map/while/body/eval_jaxpr/dot_general | solution.py:48
  14.7 2.2 %fusion.35 = f32[3,4096]{1,0:T(4,128)S(1)} fusion(f32[3,4096]{1,0:T(4,128)S(1)} %get-tuple-element.532, s32[]{:T(128)S(6)} %select_n.77, f32[3,512]{1,0:T(4,128)S(1)} %get-tuple-element.542, f32[4096,512]{1,0:T(8,128)} %get-tuple-element.541), kind=kOutput, calls=%fused_computation.3.clone.1 | convolution fusion | flops 9437184 | bytes 1065984 | tf_op jit(solution)/shard_map/while/body/eval_jaxpr/dot_general | solution.py:48
  16.9 2.2 %fusion.35 = f32[3,4096]{1,0:T(4,128)S(1)} fusion(f32[3,4096]{1,0:T(4,128)S(1)} %get-tuple-element.532, s32[]{:T(128)S(6)} %select_n.77, f32[3,512]{1,0:T(4,128)S(1)} %get-tuple-element.542, f32[4096,512]{1,0:T(8,128)} %get-tuple-element.541), kind=kOutput, calls=%fused_computation.3.clone.1 | convolution fusion | flops 9437184 | bytes 1065984 | tf_op jit(solution)/shard_map/while/body/eval_jaxpr/dot_general | solution.py:48
  19.1 10.4 %psum.21 = f32[3,4096]{1,0:T(4,128)S(1)} all-reduce(f32[3,4096]{1,0:T(4,128)S(1)} %get-tuple-element.347), channel_id=1, replica_groups=mesh['tm'=2,'loan'=8,'cov'=2] {'cov'}, use_global_device_ids=true, to_apply=%region_2.0 | all-reduce | flops 12288 | bytes 98304 | tf_op jit(solution)/shard_map/psum | solution.py:52
  31.2 3.3 %while.52 = (s32[]{:T(128)}, f32[4,256]{1,0:T(4,128)S(1)}, f32[4,4096]{1,0:T(4,128)S(1)}, s32[4096]{0:T(1024)S(1)}, s32[]{:T(128)}, /*index=5*/s32[]{:T(128)}, s32[]{:T(128)}, s32[]{:T(128)}) while((s32[]{:T(128)}, f32[4,256]{1,0:T(4,128)S(1)}, f32[4,4096]{1,0:T(4,128)S(1)}, s32[4096]{0:T(1024)S(1)}, s32[]{:T(128)}, ...), condition=%wide.region_4.0_spmd.clone, body=%wide.region_3.0_spmd.clone.sunk | while | flops 6424583 | bytes 22677 | solution.py:34
  34.5 21.6 %psum.22 = f32[4,256]{1,0:T(4,128)S(1)} all-reduce(f32[4,256]{1,0:T(4,128)S(1)} %get-tuple-element.348), channel_id=1, replica_groups=mesh['tm'=2,'loan'=8,'cov'=2] {'loan'}, use_global_device_ids=true, to_apply=%region_5.0 | all-reduce | flops 1024 | bytes 8192 | tf_op jit(solution)/shard_map/psum | solution.py:74
  58.5 2.4 %all-reduce = f32[6]{0:T(128)S(1)} all-reduce(f32[6]{0:T(128)S(1)} %dynamic-update-slice), channel_id=2, replica_groups=mesh['tm'=2,'loan'=8,'cov'=2] {'tm'}, use_global_device_ids=true, to_apply=%add | all-reduce | flops 6 | bytes 48
  61.6 2.4 %all-reduce.1 = f32[6]{0:T(128)S(1)} all-reduce(f32[6]{0:T(128)S(1)} %dynamic-update-slice.1), channel_id=3, replica_groups=mesh['tm'=2,'loan'=8,'cov'=2] {'tm'}, use_global_device_ids=true, to_apply=%add.1 | all-reduce | flops 6 | bytes 48
  64.3 19.3 %while.53 = (s32[]{:T(128)}, f32[2,512]{1,0:T(2,128)S(1)}, f32[4096]{0:T(1024)S(1)}, f32[2,4096]{1,0:T(2,128)S(1)}, s32[4096]{0:T(1024)S(1)}, /*index=5*/f32[3,2...) while((s32[]{:T(128)}, f32[2,512]{1,0:T(2,128)S(1)}, ...), condition=%wide.region_9.10_spmd.clone, body=%wide.region_8.9_spmd.clone.sunk | while | flops 11146247 | bytes 1094316 | solution.py:34
  64.9 1.9 %convolution_add_fusion.7 = f32[2,512]{1,0:T(2,128)S(1)} fusion(f32[4096,512]{1,0:T(8,128)} %get-tuple-element.599, s32[]{:T(128)S(6)} %select_n.79, f32[3,512]{1,0:T(4,128)S(1)} %convolution_bitcast_fusion.3, f32[2,512]{1,0:T(2,128)S(1)} %get-tuple-element.583, f32[2,4096]{1,0:T(2,128)S(1)} %get-tuple-element.596, pred[]{:T(512)S(6)} %compare.7, ...), kind=kOutput, calls=%fused_computation.12.clone.1 | convolution fusion | flops 6296576 | bytes 1070592 | tf_op jit(solution)/shard_map/while/body/eval_jaxpr/dot_general | solution.py:96
  67.3 1.9 %convolution_add_fusion.7 = f32[2,512]{1,0:T(2,128)S(1)} fusion(f32[4096,512]{1,0:T(8,128)} %get-tuple-element.599, s32[]{:T(128)S(6)} %select_n.79, f32[3,512]{1,0:T(4,128)S(1)} %convolution_bitcast_fusion.3, f32[2,512]{1,0:T(2,128)S(1)} %get-tuple-element.583, f32[2,4096]{1,0:T(2,128)S(1)} %get-tuple-element.596, pred[]{:T(512)S(6)} %compare.7, ...), kind=kOutput, calls=%fused_computation.12.clone.1 | convolution fusion | flops 6296576 | bytes 1070592 | tf_op jit(solution)/shard_map/while/body/eval_jaxpr/dot_general | solution.py:96
  69.7 1.9 %convolution_add_fusion.7 = f32[2,512]{1,0:T(2,128)S(1)} fusion(f32[4096,512]{1,0:T(8,128)} %get-tuple-element.599, s32[]{:T(128)S(6)} %select_n.79, f32[3,512]{1,0:T(4,128)S(1)} %convolution_bitcast_fusion.3, f32[2,512]{1,0:T(2,128)S(1)} %get-tuple-element.583, f32[2,4096]{1,0:T(2,128)S(1)} %get-tuple-element.596, pred[]{:T(512)S(6)} %compare.7, ...), kind=kOutput, calls=%fused_computation.12.clone.1 | convolution fusion | flops 6296576 | bytes 1070592 | tf_op jit(solution)/shard_map/while/body/eval_jaxpr/dot_general | solution.py:96
  72.1 1.9 %convolution_add_fusion.7 = f32[2,512]{1,0:T(2,128)S(1)} fusion(f32[4096,512]{1,0:T(8,128)} %get-tuple-element.599, s32[]{:T(128)S(6)} %select_n.79, f32[3,512]{1,0:T(4,128)S(1)} %convolution_bitcast_fusion.3, f32[2,512]{1,0:T(2,128)S(1)} %get-tuple-element.583, f32[2,4096]{1,0:T(2,128)S(1)} %get-tuple-element.596, pred[]{:T(512)S(6)} %compare.7, ...), kind=kOutput, calls=%fused_computation.12.clone.1 | convolution fusion | flops 6296576 | bytes 1070592 | tf_op jit(solution)/shard_map/while/body/eval_jaxpr/dot_general | solution.py:96
  74.5 1.9 %convolution_add_fusion.7 = f32[2,512]{1,0:T(2,128)S(1)} fusion(f32[4096,512]{1,0:T(8,128)} %get-tuple-element.599, s32[]{:T(128)S(6)} %select_n.79, f32[3,512]{1,0:T(4,128)S(1)} %convolution_bitcast_fusion.3, f32[2,512]{1,0:T(2,128)S(1)} %get-tuple-element.583, f32[2,4096]{1,0:T(2,128)S(1)} %get-tuple-element.596, pred[]{:T(512)S(6)} %compare.7, ...), kind=kOutput, calls=%fused_computation.12.clone.1 | convolution fusion | flops 6296576 | bytes 1070592 | tf_op jit(solution)/shard_map/while/body/eval_jaxpr/dot_general | solution.py:96
  76.9 1.9 %convolution_add_fusion.7 = f32[2,512]{1,0:T(2,128)S(1)} fusion(f32[4096,512]{1,0:T(8,128)} %get-tuple-element.599, s32[]{:T(128)S(6)} %select_n.79, f32[3,512]{1,0:T(4,128)S(1)} %convolution_bitcast_fusion.3, f32[2,512]{1,0:T(2,128)S(1)} %get-tuple-element.583, f32[2,4096]{1,0:T(2,128)S(1)} %get-tuple-element.596, pred[]{:T(512)S(6)} %compare.7, ...), kind=kOutput, calls=%fused_computation.12.clone.1 | convolution fusion | flops 6296576 | bytes 1070592 | tf_op jit(solution)/shard_map/while/body/eval_jaxpr/dot_general | solution.py:96
  79.3 1.9 %convolution_add_fusion.7 = f32[2,512]{1,0:T(2,128)S(1)} fusion(f32[4096,512]{1,0:T(8,128)} %get-tuple-element.599, s32[]{:T(128)S(6)} %select_n.79, f32[3,512]{1,0:T(4,128)S(1)} %convolution_bitcast_fusion.3, f32[2,512]{1,0:T(2,128)S(1)} %get-tuple-element.583, f32[2,4096]{1,0:T(2,128)S(1)} %get-tuple-element.596, pred[]{:T(512)S(6)} %compare.7, ...), kind=kOutput, calls=%fused_computation.12.clone.1 | convolution fusion | flops 6296576 | bytes 1070592 | tf_op jit(solution)/shard_map/while/body/eval_jaxpr/dot_general | solution.py:96
  81.7 1.9 %convolution_add_fusion.7 = f32[2,512]{1,0:T(2,128)S(1)} fusion(f32[4096,512]{1,0:T(8,128)} %get-tuple-element.599, s32[]{:T(128)S(6)} %select_n.79, f32[3,512]{1,0:T(4,128)S(1)} %convolution_bitcast_fusion.3, f32[2,512]{1,0:T(2,128)S(1)} %get-tuple-element.583, f32[2,4096]{1,0:T(2,128)S(1)} %get-tuple-element.596, pred[]{:T(512)S(6)} %compare.7, ...), kind=kOutput, calls=%fused_computation.12.clone.1 | convolution fusion | flops 6296576 | bytes 1070592 | tf_op jit(solution)/shard_map/while/body/eval_jaxpr/dot_general | solution.py:96
  83.6 29.5 %psum.23 = f32[2,512]{1,0:T(2,128)S(1)} all-reduce(f32[2,512]{1,0:T(2,128)S(1)} %get-tuple-element.349), channel_id=1, replica_groups=mesh['tm'=2,'loan'=8,'cov'=2] {'tm','loan'}, use_global_device_ids=true, to_apply=%region_10.11 | all-reduce | flops 1024 | bytes 8192 | tf_op jit(solution)/shard_map/psum | solution.py:99
  (72 shorter events, 13.2 us)
where the time goes:
time: 115 us; the launch traced here: 114 us
  blocking collectives  66.4 us (58%)
  matrix products  38.3 us (33%)
  local copies, waits for them, and re-layouts  4.14 us (4%)
  other arithmetic  3.32 us (3%)
  between operations  1.43 us (1%)
    psum x1, blocking collectives, per_device(): product = lax.psum(parts, ('tm', 'loan'))  29.5 us
    psum x1, blocking collectives, per_device(): totals = lax.psum(stats_local, 'loan')  21.6 us
    dot_general x8, matrix products, predict(): lax.dot_general(coeffs, piece, (((1,), (1,)), ((), ())), precision=exact_...  17.7 us
    dot_general x8, matrix products, assemble(): return product_acc + jnp.dot(resid, piece, precision=exact_mode)  14.8 us
    psum x1, blocking collectives, per_device(): linear = lax.psum(partial_value, 'cov')  10.4 us
    unnamed x2, blocking collectives  4.89 us
    dot_general x8, matrix products, assemble(): lax.dot_general(cumulative, member, (((1,), (1,)), ((), ())), precision=e...  2.98 us
    dot_general x8, matrix products, tally(): return stats_acc + jnp.dot(values, member, precision=exact_mode)  2.45 us

commit v1 on v0

--- a/solution.py
+++ b/solution.py
@@ -49,7 +49,7 @@
         return lax.dynamic_update_slice_in_dim(partial_value, values, start, 1)
 
     partial_value = sweep(trips, block, predict, jnp.zeros((3, row_total), jnp.float32))
-    linear = lax.psum(partial_value, "cov")
+    linear = jnp.sum(lax.all_gather(partial_value, "cov"), axis=0)
     valid = (jnp.arange(row_total, dtype=jnp.int32) < row_count).astype(jnp.float32)
     weight = valid * jnp.exp(linear[0])
     projected = linear[1:3]

time: 115 us -> 111 us (0.965)
  blocking collectives: 66.4 us -> 62.5 us
    psum x1 -> x0, blocking collectives: 10.4 us -> none  [per_device(): linear = lax.psum(partial_value, 'cov')]
    all_gather x0 -> x1, blocking collectives: none -> 5.87 us  [per_device(): linear = jnp.sum(lax.all_gather(partial_value, 'cov'), axis=0)]
where the time goes in v1:
time: 111 us; the launch traced here: 110 us
  blocking collectives  62.5 us (56%)
  matrix products  38.3 us (35%)
  local copies, waits for them, and re-layouts  4.14 us (4%)
  other arithmetic  3.36 us (3%)
  between operations  1.43 us (1%)
    psum x1, blocking collectives, per_device(): product = lax.psum(parts, ('tm', 'loan'))  29.5 us
    psum x1, blocking collectives, per_device(): totals = lax.psum(stats_local, 'loan')  22.3 us
    dot_general x8, matrix products, predict(): lax.dot_general(coeffs, piece, (((1,), (1,)), ((), ())), precision=exact_...  17.7 us
    dot_general x8, matrix products, assemble(): return product_acc + jnp.dot(resid, piece, precision=exact_mode)  14.8 us
    all_gather x1, blocking collectives, per_device(): linear = jnp.sum(lax.all_gather(partial_value, 'cov'), axis=0)  5.87 us
    unnamed x2, blocking collectives  4.89 us
    dot_general x8, matrix products, assemble(): lax.dot_general(cumulative, member, (((1,), (1,)), ((), ())), precision=e...  2.98 us
    dot_general x8, matrix products, tally(): return stats_acc + jnp.dot(values, member, precision=exact_mode)  2.45 us

profile of v1, /device:TPU:0, one launch (start us, length us, event | category | flops | bytes accessed | tf_op | source)
XLA Modules:
  0.0 109.8 jit_solution(14468728578998467763)
XLA Ops:
  1.4 17.8 %while.51 = (s32[]{:T(128)}, f32[3,4096]{1,0:T(4,128)S(1)}, f32[4096,512]{1,0:T(8,128)}, f32[3,512]{1,0:T(4,128)S(1)}, s32[]{:T(128)}, /*index=5*/s32[]{:T(128)}, s32[]{:T(128)}, s32[]{:T(128)}) while((s32[]{:T(128)}, f32[3,4096]{1,0:T(4,128)S(1)}, f32[4096,512]{1,0:T(8,128)}, f32[3,512]{1,0:T(4,128)S(1)}, s32[]{:T(128)}, ...), condition=%wide.region_1.0_spmd, body=%wide.region_0.0_spmd.sunk | while | flops 9437190 | bytes 1066115 | solution.py:34
  1.4 2.2 %fusion.35 = f32[3,4096]{1,0:T(4,128)S(1)} fusion(f32[3,4096]{1,0:T(4,128)S(1)} %get-tuple-element.532, s32[]{:T(128)S(6)} %select_n.77, f32[3,512]{1,0:T(4,128)S(1)} %get-tuple-element.542, f32[4096,512]{1,0:T(8,128)} %get-tuple-element.541), kind=kOutput, calls=%fused_computation.3.clone.1 | convolution fusion | flops 9437184 | bytes 1065984 | tf_op jit(solution)/shard_map/while/body/eval_jaxpr/dot_general | solution.py:48
  3.6 2.2 %fusion.35 = f32[3,4096]{1,0:T(4,128)S(1)} fusion(f32[3,4096]{1,0:T(4,128)S(1)} %get-tuple-element.532, s32[]{:T(128)S(6)} %select_n.77, f32[3,512]{1,0:T(4,128)S(1)} %get-tuple-element.542, f32[4096,512]{1,0:T(8,128)} %get-tuple-element.541), kind=kOutput, calls=%fused_computation.3.clone.1 | convolution fusion | flops 9437184 | bytes 1065984 | tf_op jit(solution)/shard_map/while/body/eval_jaxpr/dot_general | solution.py:48
  5.8 2.2 %fusion.35 = f32[3,4096]{1,0:T(4,128)S(1)} fusion(f32[3,4096]{1,0:T(4,128)S(1)} %get-tuple-element.532, s32[]{:T(128)S(6)} %select_n.77, f32[3,512]{1,0:T(4,128)S(1)} %get-tuple-element.542, f32[4096,512]{1,0:T(8,128)} %get-tuple-element.541), kind=kOutput, calls=%fused_computation.3.clone.1 | convolution fusion | flops 9437184 | bytes 1065984 | tf_op jit(solution)/shard_map/while/body/eval_jaxpr/dot_general | solution.py:48
  8.0 2.2 %fusion.35 = f32[3,4096]{1,0:T(4,128)S(1)} fusion(f32[3,4096]{1,0:T(4,128)S(1)} %get-tuple-element.532, s32[]{:T(128)S(6)} %select_n.77, f32[3,512]{1,0:T(4,128)S(1)} %get-tuple-element.542, f32[4096,512]{1,0:T(8,128)} %get-tuple-element.541), kind=kOutput, calls=%fused_computation.3.clone.1 | convolution fusion | flops 9437184 | bytes 1065984 | tf_op jit(solution)/shard_map/while/body/eval_jaxpr/dot_general | solution.py:48
  10.3 2.2 %fusion.35 = f32[3,4096]{1,0:T(4,128)S(1)} fusion(f32[3,4096]{1,0:T(4,128)S(1)} %get-tuple-element.532, s32[]{:T(128)S(6)} %select_n.77, f32[3,512]{1,0:T(4,128)S(1)} %get-tuple-element.542, f32[4096,512]{1,0:T(8,128)} %get-tuple-element.541), kind=kOutput, calls=%fused_computation.3.clone.1 | convolution fusion | flops 9437184 | bytes 1065984 | tf_op jit(solution)/shard_map/while/body/eval_jaxpr/dot_general | solution.py:48
  12.5 2.2 %fusion.35 = f32[3,4096]{1,0:T(4,128)S(1)} fusion(f32[3,4096]{1,0:T(4,128)S(1)} %get-tuple-element.532, s32[]{:T(128)S(6)} %select_n.77, f32[3,512]{1,0:T(4,128)S(1)} %get-tuple-element.542, f32[4096,512]{1,0:T(8,128)} %get-tuple-element.541), kind=kOutput, calls=%fused_computation.3.clone.1 | convolution fusion | flops 9437184 | bytes 1065984 | tf_op jit(solution)/shard_map/while/body/eval_jaxpr/dot_general | solution.py:48
  14.7 2.2 %fusion.35 = f32[3,4096]{1,0:T(4,128)S(1)} fusion(f32[3,4096]{1,0:T(4,128)S(1)} %get-tuple-element.532, s32[]{:T(128)S(6)} %select_n.77, f32[3,512]{1,0:T(4,128)S(1)} %get-tuple-element.542, f32[4096,512]{1,0:T(8,128)} %get-tuple-element.541), kind=kOutput, calls=%fused_computation.3.clone.1 | convolution fusion | flops 9437184 | bytes 1065984 | tf_op jit(solution)/shard_map/while/body/eval_jaxpr/dot_general | solution.py:48
  16.9 2.2 %fusion.35 = f32[3,4096]{1,0:T(4,128)S(1)} fusion(f32[3,4096]{1,0:T(4,128)S(1)} %get-tuple-element.532, s32[]{:T(128)S(6)} %select_n.77, f32[3,512]{1,0:T(4,128)S(1)} %get-tuple-element.542, f32[4096,512]{1,0:T(8,128)} %get-tuple-element.541), kind=kOutput, calls=%fused_computation.3.clone.1 | convolution fusion | flops 9437184 | bytes 1065984 | tf_op jit(solution)/shard_map/while/body/eval_jaxpr/dot_general | solution.py:48
  19.1 5.9 %all-gather.3 = f32[2,3,4096]{2,1,0:T(4,128)S(1)} all-gather(f32[1,3,4096]{2,1,0:T(4,128)S(1)} %bitcast.31), channel_id=2, replica_groups=mesh['tm'=2,'loan'=8,'cov'=2] {'cov'}, dimensions={0}, use_global_device_ids=true | all-gather | bytes 147456 | tf_op jit(solution)/shard_map/all_gather | solution.py:52
  26.6 3.3 %while.52 = (s32[]{:T(128)}, f32[4,256]{1,0:T(4,128)S(1)}, f32[4,4096]{1,0:T(4,128)S(1)}, s32[4096]{0:T(1024)S(1)}, s32[]{:T(128)}, /*index=5*/s32[]{:T(128)}, s32[]{:T(128)}, s32[]{:T(128)}) while((s32[]{:T(128)}, f32[4,256]{1,0:T(4,128)S(1)}, f32[4,4096]{1,0:T(4,128)S(1)}, s32[4096]{0:T(1024)S(1)}, s32[]{:T(128)}, ...), condition=%wide.region_4.0_spmd.clone, body=%wide.region_3.0_spmd.clone.sunk | while | flops 6424583 | bytes 22677 | solution.py:34
  30.0 22.3 %psum.14 = f32[4,256]{1,0:T(4,128)S(1)} all-reduce(f32[4,256]{1,0:T(4,128)S(1)} %get-tuple-element.348), channel_id=1, replica_groups=mesh['tm'=2,'loan'=8,'cov'=2] {'loan'}, use_global_device_ids=true, to_apply=%region_5.0 | all-reduce | flops 1024 | bytes 8192 | tf_op jit(solution)/shard_map/psum | solution.py:74
  54.6 2.4 %all-reduce = f32[6]{0:T(128)S(1)} all-reduce(f32[6]{0:T(128)S(1)} %dynamic-update-slice), channel_id=3, replica_groups=mesh['tm'=2,'loan'=8,'cov'=2] {'tm'}, use_global_device_ids=true, to_apply=%add | all-reduce | flops 6 | bytes 48
  57.7 2.4 %all-reduce.1 = f32[6]{0:T(128)S(1)} all-reduce(f32[6]{0:T(128)S(1)} %dynamic-update-slice.1), channel_id=4, replica_groups=mesh['tm'=2,'loan'=8,'cov'=2] {'tm'}, use_global_device_ids=true, to_apply=%add.1 | all-reduce | flops 6 | bytes 48
  60.5 19.3 %while.53 = (s32[]{:T(128)}, f32[2,512]{1,0:T(2,128)S(1)}, f32[4096]{0:T(1024)S(1)}, f32[2,4096]{1,0:T(2,128)S(1)}, s32[4096]{0:T(1024)S(1)}, /*index=5*/f32[3,2...) while((s32[]{:T(128)}, f32[2,512]{1,0:T(2,128)S(1)}, ...), condition=%wide.region_9.10_spmd.clone, body=%wide.region_8.9_spmd.clone.sunk | while | flops 11146247 | bytes 1094316 | solution.py:34
  61.0 1.9 %convolution_add_fusion.7 = f32[2,512]{1,0:T(2,128)S(1)} fusion(f32[4096,512]{1,0:T(8,128)} %get-tuple-element.599, s32[]{:T(128)S(6)} %select_n.79, f32[3,512]{1,0:T(4,128)S(1)} %convolution_bitcast_fusion.3, f32[2,512]{1,0:T(2,128)S(1)} %get-tuple-element.583, f32[2,4096]{1,0:T(2,128)S(1)} %get-tuple-element.596, pred[]{:T(512)S(6)} %compare.7, ...), kind=kOutput, calls=%fused_computation.12.clone.1 | convolution fusion | flops 6296576 | bytes 1070592 | tf_op jit(solution)/shard_map/while/body/eval_jaxpr/dot_general | solution.py:96
  63.4 1.9 %convolution_add_fusion.7 = f32[2,512]{1,0:T(2,128)S(1)} fusion(f32[4096,512]{1,0:T(8,128)} %get-tuple-element.599, s32[]{:T(128)S(6)} %select_n.79, f32[3,512]{1,0:T(4,128)S(1)} %convolution_bitcast_fusion.3, f32[2,512]{1,0:T(2,128)S(1)} %get-tuple-element.583, f32[2,4096]{1,0:T(2,128)S(1)} %get-tuple-element.596, pred[]{:T(512)S(6)} %compare.7, ...), kind=kOutput, calls=%fused_computation.12.clone.1 | convolution fusion | flops 6296576 | bytes 1070592 | tf_op jit(solution)/shard_map/while/body/eval_jaxpr/dot_general | solution.py:96
  65.8 1.9 %convolution_add_fusion.7 = f32[2,512]{1,0:T(2,128)S(1)} fusion(f32[4096,512]{1,0:T(8,128)} %get-tuple-element.599, s32[]{:T(128)S(6)} %select_n.79, f32[3,512]{1,0:T(4,128)S(1)} %convolution_bitcast_fusion.3, f32[2,512]{1,0:T(2,128)S(1)} %get-tuple-element.583, f32[2,4096]{1,0:T(2,128)S(1)} %get-tuple-element.596, pred[]{:T(512)S(6)} %compare.7, ...), kind=kOutput, calls=%fused_computation.12.clone.1 | convolution fusion | flops 6296576 | bytes 1070592 | tf_op jit(solution)/shard_map/while/body/eval_jaxpr/dot_general | solution.py:96
  68.3 1.9 %convolution_add_fusion.7 = f32[2,512]{1,0:T(2,128)S(1)} fusion(f32[4096,512]{1,0:T(8,128)} %get-tuple-element.599, s32[]{:T(128)S(6)} %select_n.79, f32[3,512]{1,0:T(4,128)S(1)} %convolution_bitcast_fusion.3, f32[2,512]{1,0:T(2,128)S(1)} %get-tuple-element.583, f32[2,4096]{1,0:T(2,128)S(1)} %get-tuple-element.596, pred[]{:T(512)S(6)} %compare.7, ...), kind=kOutput, calls=%fused_computation.12.clone.1 | convolution fusion | flops 6296576 | bytes 1070592 | tf_op jit(solution)/shard_map/while/body/eval_jaxpr/dot_general | solution.py:96
  70.7 1.9 %convolution_add_fusion.7 = f32[2,512]{1,0:T(2,128)S(1)} fusion(f32[4096,512]{1,0:T(8,128)} %get-tuple-element.599, s32[]{:T(128)S(6)} %select_n.79, f32[3,512]{1,0:T(4,128)S(1)} %convolution_bitcast_fusion.3, f32[2,512]{1,0:T(2,128)S(1)} %get-tuple-element.583, f32[2,4096]{1,0:T(2,128)S(1)} %get-tuple-element.596, pred[]{:T(512)S(6)} %compare.7, ...), kind=kOutput, calls=%fused_computation.12.clone.1 | convolution fusion | flops 6296576 | bytes 1070592 | tf_op jit(solution)/shard_map/while/body/eval_jaxpr/dot_general | solution.py:96
  73.1 1.9 %convolution_add_fusion.7 = f32[2,512]{1,0:T(2,128)S(1)} fusion(f32[4096,512]{1,0:T(8,128)} %get-tuple-element.599, s32[]{:T(128)S(6)} %select_n.79, f32[3,512]{1,0:T(4,128)S(1)} %convolution_bitcast_fusion.3, f32[2,512]{1,0:T(2,128)S(1)} %get-tuple-element.583, f32[2,4096]{1,0:T(2,128)S(1)} %get-tuple-element.596, pred[]{:T(512)S(6)} %compare.7, ...), kind=kOutput, calls=%fused_computation.12.clone.1 | convolution fusion | flops 6296576 | bytes 1070592 | tf_op jit(solution)/shard_map/while/body/eval_jaxpr/dot_general | solution.py:96
  75.5 1.9 %convolution_add_fusion.7 = f32[2,512]{1,0:T(2,128)S(1)} fusion(f32[4096,512]{1,0:T(8,128)} %get-tuple-element.599, s32[]{:T(128)S(6)} %select_n.79, f32[3,512]{1,0:T(4,128)S(1)} %convolution_bitcast_fusion.3, f32[2,512]{1,0:T(2,128)S(1)} %get-tuple-element.583, f32[2,4096]{1,0:T(2,128)S(1)} %get-tuple-element.596, pred[]{:T(512)S(6)} %compare.7, ...), kind=kOutput, calls=%fused_computation.12.clone.1 | convolution fusion | flops 6296576 | bytes 1070592 | tf_op jit(solution)/shard_map/while/body/eval_jaxpr/dot_general | solution.py:96
  77.9 1.9 %convolution_add_fusion.7 = f32[2,512]{1,0:T(2,128)S(1)} fusion(f32[4096,512]{1,0:T(8,128)} %get-tuple-element.599, s32[]{:T(128)S(6)} %select_n.79, f32[3,512]{1,0:T(4,128)S(1)} %convolution_bitcast_fusion.3, f32[2,512]{1,0:T(2,128)S(1)} %get-tuple-element.583, f32[2,4096]{1,0:T(2,128)S(1)} %get-tuple-element.596, pred[]{:T(512)S(6)} %compare.7, ...), kind=kOutput, calls=%fused_computation.12.clone.1 | convolution fusion | flops 6296576 | bytes 1070592 | tf_op jit(solution)/shard_map/while/body/eval_jaxpr/dot_general | solution.py:96
  79.7 29.5 %psum.15 = f32[2,512]{1,0:T(2,128)S(1)} all-reduce(f32[2,512]{1,0:T(2,128)S(1)} %get-tuple-element.349), channel_id=1, replica_groups=mesh['tm'=2,'loan'=8,'cov'=2] {'tm','loan'}, use_global_device_ids=true, to_apply=%region_10.11 | all-reduce | flops 1024 | bytes 8192 | tf_op jit(solution)/shard_map/psum | solution.py:99
  (73 shorter events, 13.3 us)
